TPU v7x, 128 devices: a whole 4x4x4 slice. The times are simulated.
128 devices in a mesh: tile: 32 (over z, y, core), frame: 4 (over x).
Axes of the slice: x: 4, y: 4, z: 4, core: 2. Of those that a mesh axis runs over, the one named last changes fastest.
Arguments:
- movie: bfloat16 [128, 2048, 256], P(('frame', 'tile')), may hold values from -6 to 6
- footprints: bfloat16 [2048, 256, 384], P('tile'), may hold values from -0.09375 to 0.09375
- support: int32 [256, 384], P('tile'), may hold values 0 or 1
- traces: bfloat16 [12288, 128], P('tile', 'frame'), may hold values from 0 to 2
- border_weight: float32 [2048, 256], P('tile'), may hold values from 1 to 4
- border_offsets: int32 [64, 2], replicated, may hold values from -16 to 16, as said below
Outputs:
- new_traces: float32 [12288, 128], P('tile', 'frame')
- trace_gram: float32 [12288, 384], P('tile')
- remainder: bfloat16 [128, 2048, 256], P(('frame', 'tile'))
Inputs may be any that keep to these rules, and one draw needn't show every extreme that they name: `border_offsets`: the 64 rows are distinct offsets (row, column) on the boundary of the square of half-side 16; (-16, -16) and (16, 16) are among them.
All inputs are finite; a program needn't handle non-finite values. No bound on the sum of `support` on one device may be relied on, other than what follows from the above.
Results may differ from a plain program's by a relative error of at most 0.009.
Values may be sent and summed in bfloat16 or wider, within the bound.
A program may use at most 128 MiB of HBM per device.

v0:
```python
import functools
import math

import jax
import jax.numpy as jnp
import numpy as np
from jax import lax
from jax.experimental import pallas as pl
from jax.experimental.pallas import tpu as pltpu
from jax.sharding import PartitionSpec as P

RR = 16
GR = 4
BR = 8
SWEEPS = 3
NR = 64
TH = 64
W = 256
KT = 384
HB = 32
NBLOCK = TH // BR
CHUNKS = 4
CROWS = TH // CHUNKS
F32 = jnp.float32
BF16 = jnp.bfloat16

_raw = np.exp(-2.0 * np.arange(-GR, GR + 1, dtype=np.float32) ** 2 / np.float32(GR * GR)).astype(np.float32)
TAPS = _raw / _raw.sum(dtype=np.float32)


def tap(d):
    away = jnp.abs(d)
    value = jnp.zeros(d.shape, F32)
    for step in range(GR + 1):
        value = jnp.where(away == step, float(TAPS[GR + step]), value)
    return value


def dot(a, b):
    return jnp.dot(a, b, preferred_element_type=F32)


def dot_nt(a, b):
    return lax.dot_general(a, b, (((1,), (1,)), ((), ())), preferred_element_type=F32)


def dot_tn(a, b):
    return lax.dot_general(a, b, (((0,), (0,)), ((), ())), preferred_element_type=F32)


def split(a):
    high = a.astype(BF16)
    return high, (a - high.astype(F32)).astype(BF16)


def build_operators(me, tiles, offs, rmat, cmat):
    rows_of, cols_of = offs[0:1, :], offs[1:2, :]
    place = lax.broadcasted_iota(jnp.int32, (128, NR), 0) - RR
    col_hot = (place == cols_of).astype(F32)
    row_hot = (place == rows_of).astype(F32)
    inner = jnp.abs(rows_of) < RR
    which = lax.broadcasted_iota(jnp.int32, (8, NR), 0)
    side_rows = jnp.where(which == 0, rows_of, jnp.where(which == 1, rows_of, 99))
    is_row = ((which == 0) & (side_rows == -RR)) | ((which == 1) & (side_rows == RR))
    is_col = inner & (((which == 0) & (cols_of == -RR)) | ((which == 1) & (cols_of == RR)))
    row_sides = dot_nt(is_row.astype(F32), col_hot)
    col_sides = dot_nt(is_col.astype(F32), row_hot)

    u = lax.broadcasted_iota(jnp.int32, (W, W), 0)
    x = lax.broadcasted_iota(jnp.int32, (W, W), 1)
    gap = u - x
    smooth_high, smooth_low = split(tap(gap))
    for side in range(2):
        band = jnp.zeros((W, W), F32)
        for b in range(-RR, RR + 1):
            band = jnp.where(gap == b, row_sides[side : side + 1, b + RR : b + RR + 1], band)
        band = band.astype(BF16)
        cmat[side * W : (side + 1) * W, :] = (dot(smooth_high, band) + dot(smooth_low, band)).astype(BF16)
        shift = RR if side == 0 else -RR
        source = x - shift
        kept = (source >= 0) & (source < W)
        cmat[(2 + side) * W : (3 + side) * W, :] = jnp.where(kept, tap(u - source), 0.0).astype(BF16)

    total_rows = tiles * TH
    y = lax.broadcasted_iota(jnp.int32, (TH, 128), 0)
    v = lax.broadcasted_iota(jnp.int32, (TH, 128), 1)
    rel = jnp.where(v < TH, v, jnp.where(v < TH + HB, v - (TH + HB), v - HB))

    def inside(row):
        place_of = row + me * TH
        return (place_of >= 0) & (place_of < total_rows)

    seen = inside(rel)
    parts = []
    for a in (-RR, RR):
        parts.append(jnp.where(seen & inside(y + a), tap(rel - y - a), 0.0))
    left = jnp.zeros((TH, 128), F32)
    right = jnp.zeros((TH, 128), F32)
    for a in range(-RR + 1, RR):
        term = jnp.where(seen & inside(y + a), tap(rel - y - a), 0.0)
        left = left + term * col_sides[0:1, a + RR : a + RR + 1]
        right = right + term * col_sides[1:2, a + RR : a + RR + 1]
    for index, part in enumerate(parts + [left, right]):
        high, low = split(part)
        rmat[index * TH : (index + 1) * TH, 0:128] = high
        rmat[index * TH : (index + 1) * TH, 128:256] = low


def kernel(
    tiles, slabs, movie, foot, support, traces, weight, offs, out_traces, out_gram, out_rest,
    shaped, strips, flat, first, above, below, cmat, rmat, stage, cleaned, coupling, rest, gathered,
    load_sem, in_send, in_recv, halo_send, halo_recv, gram_send, gram_recv, out_send, out_recv,
):
    me = lax.axis_index("tile")
    slab = lax.axis_index("frame")
    frames = tiles
    group = min(8, frames)
    groups = frames // group

    barrier = pltpu.get_barrier_semaphore()

    @pl.loop(1, tiles)
    def _(step):
        pl.semaphore_signal(barrier, inc=1, device_id={"tile": lax.rem(me + step, tiles)})

    for step in range(1, slabs):
        pl.semaphore_signal(barrier, inc=1, device_id={"frame": lax.rem(slab + step, slabs)})

    for block in range(NBLOCK):
        span = pl.ds(block * BR, BR)
        pltpu.make_async_copy(foot.at[span], shaped.at[span], load_sem.at[block]).start()

    build_operators(me, tiles, offs, rmat, cmat)

    @pl.when(me == 0)
    def _():
        above[...] = jnp.zeros(above.shape, BF16)

    @pl.when(me == tiles - 1)
    def _():
        below[...] = jnp.zeros(below.shape, BF16)

    pl.semaphore_wait(barrier, tiles - 1 + slabs - 1)

    def movie_copy(peer):
        return pltpu.make_async_remote_copy(
            src_ref=movie.at[0, pl.ds(pl.multiple_of(peer * TH, TH), TH), :],
            dst_ref=strips.at[me],
            send_sem=in_send,
            recv_sem=in_recv.at[me],
            device_id={"tile": peer},
        )

    @pl.loop(1, tiles)
    def _(step):
        movie_copy(lax.rem(me + step, tiles)).start()

    pltpu.make_async_copy(
        movie.at[0, pl.ds(pl.multiple_of(me * TH, TH), TH), :], strips.at[me], in_recv.at[me]
    ).start()

    coupling[...] = jnp.zeros(coupling.shape, F32)
    old = traces[...]

    @pl.loop(0, NBLOCK)
    def _(block):
        span = pl.ds(block * BR, BR)
        pltpu.make_async_copy(foot.at[span], shaped.at[span], load_sem.at[block]).wait()
        mask = support[pl.ds(block, 1), :].astype(F32).astype(BF16)
        for inner in range(BR):
            row = block * BR + inner
            masked = shaped[row] * mask
            shaped[row] = masked
            fit = dot_nt(old, masked)
            at = pl.ds(pl.multiple_of(row * frames, frames), frames)
            flat[0, at, :] = fit[:, 0:128]
            flat[1, at, :] = fit[:, 128:256]
        pixels = shaped[span].reshape(BR * W, KT)
        coupling[...] += dot_tn(pixels, pixels)

    def halo_up(g):
        span = pl.ds(g * group, group)
        return pltpu.make_async_remote_copy(
            src_ref=first.at[span, pl.ds(0, HB), :],
            dst_ref=below.at[span],
            send_sem=halo_send.at[0, g],
            recv_sem=halo_recv.at[0, g],
            device_id={"tile": lax.max(me - 1, 0)},
        )

    def halo_down(g):
        span = pl.ds(g * group, group)
        return pltpu.make_async_remote_copy(
            src_ref=first.at[span, pl.ds(TH - HB, HB), :],
            dst_ref=above.at[span],
            send_sem=halo_send.at[1, g],
            recv_sem=halo_recv.at[1, g],
            device_id={"tile": lax.min(me + 1, tiles - 1)},
        )

    for g in range(groups):

        @pl.loop(0, group)
        def _(inner):
            f = g * group + inner
            pltpu.make_async_copy(strips.at[f], strips.at[f], in_recv.at[f]).wait()
            seen = strips[f].astype(F32)
            at = pl.ds(f, TH, stride=frames)
            first[f, :, 0:128] = (seen[:, 0:128] - flat[0, at, :]).astype(BF16)
            first[f, :, 128:256] = (seen[:, 128:256] - flat[1, at, :]).astype(BF16)

        @pl.when(me > 0)
        def _():
            halo_up(g).start()

        @pl.when(me < tiles - 1)
        def _():
            halo_down(g).start()

    for g in range(groups):

        @pl.when(me > 0)
        def _():
            halo_down(g).wait_recv()

        @pl.when(me < tiles - 1)
        def _():
            halo_up(g).wait_recv()

        @pl.loop(0, group)
        def _(inner):
            f = g * group + inner
            window = jnp.concatenate([first[f], above[f], below[f]], axis=0)
            filtered = dot(rmat[...], jnp.concatenate([window, window], axis=0))
            at = pl.ds(pl.multiple_of(inner * TH, TH), TH)
            for side in range(4):
                stage[at, side * W : (side + 1) * W] = filtered[side * TH : (side + 1) * TH].astype(BF16)

        ring = dot(stage[...], cmat[...])
        scale = weight[...] / math.sqrt(NR)
        for inner in range(group):
            f = g * group + inner
            clean = strips[f].astype(F32) - scale * ring[inner * TH : (inner + 1) * TH]
            clean = clean.astype(BF16).astype(F32)
            at = pl.ds(f, TH, stride=frames)
            cleaned[0, at, :] = clean[:, 0:128]
            cleaned[1, at, :] = clean[:, 128:256]

    def project(row, total):
        at = pl.ds(pl.multiple_of(row * frames, frames), frames)
        pixels = jnp.concatenate([cleaned[0, at, :], cleaned[1, at, :]], axis=1).astype(BF16)
        return total + dot(pixels, shaped[row])

    def project_block(block, total):
        for inner in range(BR):
            total = project(block * BR + inner, total)
        return total

    projected = lax.fori_loop(0, NBLOCK, project_block, jnp.zeros((frames, KT), F32))

    matrix = coupling[...]
    here = lax.broadcasted_iota(jnp.int32, (KT, KT), 0) == lax.broadcasted_iota(jnp.int32, (KT, KT), 1)
    floor = jnp.maximum(jnp.sum(jnp.where(here, matrix, 0.0), axis=0, keepdims=True), 1.0)
    matrix_high, matrix_low = split(matrix)
    state = old.astype(F32)
    for _ in range(SWEEPS):
        high, low = split(state)
        moved = dot(high, matrix_high) + (dot(high, matrix_low) + dot(low, matrix_high))
        state = jnp.maximum(state + (projected - moved) / floor, 0.0)
    out_traces[...] = state
    new = state.astype(BF16)
    gathered[slab] = new

    def gram_copy(peer):
        return pltpu.make_async_remote_copy(
            src_ref=gathered.at[slab],
            dst_ref=gathered.at[slab],
            send_sem=gram_send.at[peer],
            recv_sem=gram_recv.at[slab],
            device_id={"frame": peer},
        )

    for step in range(1, slabs):
        gram_copy(lax.rem(slab + step, slabs)).start()

    def rest_copy(peer, chunk):
        return pltpu.make_async_remote_copy(
            src_ref=rest.at[peer, pl.ds(pl.multiple_of(chunk * CROWS, CROWS), CROWS), :],
            dst_ref=out_rest.at[pl.ds(pl.multiple_of(me * TH + chunk * CROWS, CROWS), CROWS), :],
            send_sem=out_send,
            recv_sem=out_recv,
            device_id={"tile": peer},
        )

    @pl.loop(0, CHUNKS)
    def _(chunk):
        @pl.loop(0, CROWS // 4)
        def _(part):
            for inner in range(4):
                row = chunk * CROWS + part * 4 + inner
                at = pl.ds(pl.multiple_of(row * frames, frames), frames)
                refit = dot_nt(new, shaped[row])
                flat[0, at, :] = cleaned[0, at, :] - refit[:, 0:128]
                flat[1, at, :] = cleaned[1, at, :] - refit[:, 128:256]

        @pl.loop(0, frames)
        def _(f):
            at = pl.ds(chunk * (CROWS * frames) + f, CROWS, stride=frames)
            rows = pl.ds(pl.multiple_of(chunk * CROWS, CROWS), CROWS)
            rest[f, rows, 0:128] = flat[0, at, :].astype(BF16)
            rest[f, rows, 128:256] = flat[1, at, :].astype(BF16)

        @pl.loop(1, tiles)
        def _(step):
            rest_copy(lax.rem(me + step, tiles), chunk).start()

    out_rest[pl.ds(pl.multiple_of(me * TH, TH), TH), :] = rest[me]

    for step in range(1, slabs):
        peer = lax.rem(slab + step, slabs)
        pltpu.make_async_copy(gathered.at[peer], gathered.at[peer], gram_recv.at[peer]).wait()
    whole = gathered[...].reshape(slabs * frames, KT)
    out_gram[...] = dot_tn(whole, whole)

    for step in range(1, slabs):
        gram_copy(lax.rem(slab + step, slabs)).wait_send()
    for g in range(groups):

        @pl.when(me > 0)
        def _():
            halo_up(g).wait_send()

        @pl.when(me < tiles - 1)
        def _():
            halo_down(g).wait_send()

    others = pl.ds(0, (tiles - 1) * TH)
    everything = out_rest.at[others, :]
    pltpu.make_async_copy(movie.at[0, others, :], movie.at[0, others, :], in_send).wait()
    pltpu.make_async_copy(everything, everything, out_send).wait()
    pltpu.make_async_copy(everything, everything, out_recv).wait()


def solution(mesh):
    tiles, slabs = mesh.shape["tile"], mesh.shape["frame"]
    frames = tiles
    group = min(8, frames)
    groups = frames // group

    def per_device(movie, footprints, support, traces, border_weight, border_offsets):
        vmem = pl.BlockSpec(memory_space=pltpu.VMEM)
        hbm = pl.BlockSpec(memory_space=pl.ANY)
        state, gram, rest = pl.pallas_call(
            functools.partial(kernel, tiles, slabs),
            out_shape=(
                jax.ShapeDtypeStruct((frames, KT), F32),
                jax.ShapeDtypeStruct((KT, KT), F32),
                jax.ShapeDtypeStruct((tiles * TH, W), BF16),
            ),
            in_specs=[hbm, hbm, vmem, vmem, vmem, vmem],
            out_specs=(vmem, vmem, vmem),
            scratch_shapes=[
                pltpu.VMEM((TH, W, KT), BF16),
                pltpu.VMEM((frames, TH, W), BF16),
                pltpu.VMEM((2, TH * frames, 128), F32),
                pltpu.VMEM((frames, TH, W), BF16),
                pltpu.VMEM((frames, HB, W), BF16),
                pltpu.VMEM((frames, HB, W), BF16),
                pltpu.VMEM((4 * W, W), BF16),
                pltpu.VMEM((4 * TH, 256), BF16),
                pltpu.VMEM((group * TH, 4 * W), BF16),
                pltpu.VMEM((2, TH * frames, 128), F32),
                pltpu.VMEM((KT, KT), F32),
                pltpu.VMEM((frames, TH, W), BF16),
                pltpu.VMEM((slabs, frames, KT), BF16),
                pltpu.SemaphoreType.DMA((NBLOCK,)),
                pltpu.SemaphoreType.DMA,
                pltpu.SemaphoreType.DMA((frames,)),
                pltpu.SemaphoreType.DMA((2, groups)),
                pltpu.SemaphoreType.DMA((2, groups)),
                pltpu.SemaphoreType.DMA((slabs,)),
                pltpu.SemaphoreType.DMA((slabs,)),
                pltpu.SemaphoreType.DMA,
                pltpu.SemaphoreType.DMA,
            ],
            compiler_params=pltpu.CompilerParams(
                collective_id=0, has_side_effects=True, vmem_limit_bytes=56 * 1024 * 1024
            ),
            name="alternation",
        )(movie, footprints, support, traces.T, border_weight, border_offsets.T)
        return state.T, gram, rest[None]

    return jax.shard_map(
        per_device,
        mesh=mesh,
        in_specs=(
            P(("frame", "tile"), None, None),
            P("tile", None, None),
            P("tile", None),
            P("tile", "frame"),
            P("tile", None),
            P(),
        ),
        out_specs=(P("tile", "frame"), P("tile", None), P(("frame", "tile"), None, None)),
        check_vma=False,
    )
```

profile of v0, /device:TPU:1, one launch (start us, length us, event | category | flops | bytes accessed | tf_op | source)
XLA Modules:
  0.0 65.6 jit_solution(4623609683248685912)
XLA Ops:
  0.6 59.4 %alternation.1 = (f32[32,384]{1,0:T(8,128)}, f32[384,384]{1,0:T(8,128)}, bf16[2048,256]{1,0:T(8,128)(2,1)}) custom-call(bf16[1,2048,256]{2,1,0:T(8,128)(2,1)} %movie.1, bf16[64,256,384]{2,1,0:T(8,128)(2,1)} %foot.1, s32[8,384]{1,0:T(8,128)} %support.1, bf16[32,384]{1,0:T(8,128)(2,1)} %bitcast.6, f32[64,256]{1,0:T(8,128)} %weight.1, s32[2,64]{1,0:T(2,128)} %bitcast.7), custom_call_target="tpu_custom_call" | custom-call | tf_op jit(solution)/shard_map/alternation/pallas_call | solution.py:353
  60.0 1.4 %copy.12 = f32[384,32]{0,1:T(8,128)} copy(f32[384,32]{0,1:T(8,128)} %bitcast.5) | data formatting | bytes 98304
  61.5 1.9 %copy.13 = f32[384,384]{1,0:T(8,128)} copy(f32[384,384]{1,0:T(8,128)} %get-tuple-element.13) | data formatting | bytes 1179648
  63.4 2.3 %copy.14 = bf16[1,2048,256]{2,1,0:T(8,128)(2,1)} copy(bf16[1,2048,256]{2,1,0:T(8,128)(2,1)} %bitcast.4) | data formatting | bytes 2097152
where the time goes:
time: 65.9 us; the launch traced here: 65.6 us
  Pallas kernels  59.4 us (90%)
  local copies, waits for them, and re-layouts  5.6 us (8%)
    pallas_call x1, Pallas kernels, per_device(): pl.pallas_call(functools.partial(kernel, tiles, slabs), out_shape=(jax.Sh...  59.4 us
    unnamed x3, local copies, waits for them, and re-layouts  5.6 us

commit v1 on v0

--- a/solution.py
+++ b/solution.py
@@ -106,6 +106,14 @@
         rmat[index * TH : (index + 1) * TH, 128:256] = low
 
 
+def far_first(planes):
+    def hops(distance, size):
+        return min(distance, size - distance)
+
+    every = [(dz, dy, dc) for dz in range(planes) for dy in range(4) for dc in range(2)]
+    return sorted(every[1:], key=lambda o: -hops(o[0], planes) - hops(o[1], 4))
+
+
 def kernel(
     tiles, slabs, movie, foot, support, traces, weight, offs, out_traces, out_gram, out_rest,
     shaped, strips, flat, first, above, below, cmat, rmat, stage, cleaned, coupling, rest, gathered,
@@ -130,17 +138,16 @@
         span = pl.ds(block * BR, BR)
         pltpu.make_async_copy(foot.at[span], shaped.at[span], load_sem.at[block]).start()
 
-    build_operators(me, tiles, offs, rmat, cmat)
-
-    @pl.when(me == 0)
-    def _():
-        above[...] = jnp.zeros(above.shape, BF16)
-
-    @pl.when(me == tiles - 1)
-    def _():
-        below[...] = jnp.zeros(below.shape, BF16)
-
     pl.semaphore_wait(barrier, tiles - 1 + slabs - 1)
+
+    plane, line, core = me // 8, (me // 2) % 4, me % 2
+    planes = tiles // 8
+
+    def peer_at(offset):
+        dz, dy, dc = offset
+        return lax.rem(plane + dz, planes) * 8 + lax.rem(line + dy, 4) * 2 + lax.rem(core + dc, 2)
+
+    offsets = far_first(planes)
 
     def movie_copy(peer):
         return pltpu.make_async_remote_copy(
@@ -151,13 +158,22 @@
             device_id={"tile": peer},
         )
 
-    @pl.loop(1, tiles)
-    def _(step):
-        movie_copy(lax.rem(me + step, tiles)).start()
+    for offset in offsets:
+        movie_copy(peer_at(offset)).start()
 
     pltpu.make_async_copy(
         movie.at[0, pl.ds(pl.multiple_of(me * TH, TH), TH), :], strips.at[me], in_recv.at[me]
     ).start()
+
+    @pl.when(me == 0)
+    def _():
+        above[...] = jnp.zeros(above.shape, BF16)
+
+    @pl.when(me == tiles - 1)
+    def _():
+        below[...] = jnp.zeros(below.shape, BF16)
+
+    build_operators(me, tiles, offs, rmat, cmat)
 
     coupling[...] = jnp.zeros(coupling.shape, F32)
     old = traces[...]
@@ -198,7 +214,10 @@
             device_id={"tile": lax.min(me + 1, tiles - 1)},
         )
 
-    for g in range(groups):
+    steps = sorted(range(planes), key=lambda d: -min(d, planes - d))
+
+    for dz in steps:
+        g = lax.rem(plane + planes - dz, planes)
 
         @pl.loop(0, group)
         def _(inner):
@@ -217,7 +236,9 @@
         def _():
             halo_down(g).start()
 
-    for g in range(groups):
+    scale = weight[...] / math.sqrt(NR)
+    for dz in steps:
+        g = lax.rem(plane + planes - dz, planes)
 
         @pl.when(me > 0)
         def _():
@@ -227,17 +248,16 @@
         def _():
             halo_up(g).wait_recv()
 
-        @pl.loop(0, group)
-        def _(inner):
+        for inner in range(group):
             f = g * group + inner
             window = jnp.concatenate([first[f], above[f], below[f]], axis=0)
             filtered = dot(rmat[...], jnp.concatenate([window, window], axis=0))
-            at = pl.ds(pl.multiple_of(inner * TH, TH), TH)
             for side in range(4):
-                stage[at, side * W : (side + 1) * W] = filtered[side * TH : (side + 1) * TH].astype(BF16)
+                stage[inner * TH : (inner + 1) * TH, side * W : (side + 1) * W] = filtered[
+                    side * TH : (side + 1) * TH
+                ].astype(BF16)
 
         ring = dot(stage[...], cmat[...])
-        scale = weight[...] / math.sqrt(NR)
         for inner in range(group):
             f = g * group + inner
             clean = strips[f].astype(F32) - scale * ring[inner * TH : (inner + 1) * TH]
@@ -261,12 +281,14 @@
     matrix = coupling[...]
     here = lax.broadcasted_iota(jnp.int32, (KT, KT), 0) == lax.broadcasted_iota(jnp.int32, (KT, KT), 1)
     floor = jnp.maximum(jnp.sum(jnp.where(here, matrix, 0.0), axis=0, keepdims=True), 1.0)
-    matrix_high, matrix_low = split(matrix)
+    inverse = 1.0 / floor
+    high, low = split(jnp.where(here, 1.0, 0.0) - matrix * inverse)
+    step_matrix = jnp.concatenate([high, high, low], axis=0)
+    drive = projected / floor
     state = old.astype(F32)
     for _ in range(SWEEPS):
         high, low = split(state)
-        moved = dot(high, matrix_high) + (dot(high, matrix_low) + dot(low, matrix_high))
-        state = jnp.maximum(state + (projected - moved) / floor, 0.0)
+        state = jnp.maximum(dot(jnp.concatenate([high, low, high], axis=1), step_matrix) + drive, 0.0)
     out_traces[...] = state
     new = state.astype(BF16)
     gathered[slab] = new
@@ -310,9 +332,8 @@
             rest[f, rows, 0:128] = flat[0, at, :].astype(BF16)
             rest[f, rows, 128:256] = flat[1, at, :].astype(BF16)
 
-        @pl.loop(1, tiles)
-        def _(step):
-            rest_copy(lax.rem(me + step, tiles), chunk).start()
+        for offset in offsets:
+            rest_copy(peer_at(offset), chunk).start()
 
     out_rest[pl.ds(pl.multiple_of(me * TH, TH), TH), :] = rest[me]
 
@@ -339,6 +360,15 @@
     pltpu.make_async_copy(movie.at[0, others, :], movie.at[0, others, :], in_send).wait()
     pltpu.make_async_copy(everything, everything, out_send).wait()
     pltpu.make_async_copy(everything, everything, out_recv).wait()
+
+
+def write_out(state, gram, rest, out_state, out_gram, out_rest, sems):
+    pairs = ((rest, out_rest), (gram, out_gram), (state, out_state))
+    copies = [pltpu.make_async_copy(a, b, sems.at[i]) for i, (a, b) in enumerate(pairs)]
+    for copy in copies:
+        copy.start()
+    for copy in copies:
+        copy.wait()
 
 
 def solution(mesh):
@@ -353,9 +383,9 @@
         state, gram, rest = pl.pallas_call(
             functools.partial(kernel, tiles, slabs),
             out_shape=(
-                jax.ShapeDtypeStruct((frames, KT), F32),
-                jax.ShapeDtypeStruct((KT, KT), F32),
-                jax.ShapeDtypeStruct((tiles * TH, W), BF16),
+                pltpu.VMEM((frames, KT), F32),
+                pltpu.VMEM((KT, KT), F32),
+                pltpu.VMEM((tiles * TH, W), BF16),
             ),
             in_specs=[hbm, hbm, vmem, vmem, vmem, vmem],
             out_specs=(vmem, vmem, vmem),
@@ -388,6 +418,18 @@
             ),
             name="alternation",
         )(movie, footprints, support, traces.T, border_weight, border_offsets.T)
+        state, gram, rest = pl.pallas_call(
+            write_out,
+            out_shape=(
+                jax.ShapeDtypeStruct(state.shape, F32),
+                jax.ShapeDtypeStruct(gram.shape, F32),
+                jax.ShapeDtypeStruct(rest.shape, BF16),
+            ),
+            in_specs=[vmem, vmem, vmem],
+            out_specs=(hbm, hbm, hbm),
+            scratch_shapes=[pltpu.SemaphoreType.DMA((3,))],
+            name="write_out",
+        )(*[pltpu.with_memory_space_constraint(r, pltpu.VMEM) for r in (state, gram, rest)])
         return state.T, gram, rest[None]
 
     return jax.shard_map(

time: 65.9 us -> 55.6 us (0.84)
  local copies, waits for them, and re-layouts: 5.6 us -> 0 us
  Pallas kernels: 59.4 us -> 54.8 us
    unnamed x3 -> x0, local copies, waits for them, and re-layouts: 5.6 us -> none
    pallas_call x1 -> x2, Pallas kernels: 59.4 us -> 54.8 us  [the longest x1 53.6 us: per_device(): pl.pallas_call(functools.partial(kernel, tiles, slabs), out_shape=(pltpu....]
where the time goes in v1:
time: 55.6 us; the launch traced here: 55.4 us
  Pallas kernels  54.8 us (99%)
  between operations  0.64 us (1%)
    pallas_call x1, Pallas kernels, per_device(): pl.pallas_call(functools.partial(kernel, tiles, slabs), out_shape=(pltpu....  53.6 us
    pallas_call x1, Pallas kernels, per_device(): pl.pallas_call(write_out, out_shape=(jax.ShapeDtypeStruct(state.shape, F3...  1.19 us

profile of v1, /device:TPU:1, one launch (start us, length us, event | category | flops | bytes accessed | tf_op | source)
XLA Modules:
  0.0 55.4 jit_solution(5046743101688447603)
XLA Ops:
  0.6 53.6 %alternation.1 = (f32[32,384]{1,0:T(8,128)S(1)}, f32[384,384]{1,0:T(8,128)S(1)}, bf16[2048,256]{1,0:T(8,128)(2,1)S(1)}) custom-call(bf16[1,2048,256]{2,1,0:T(8,128)(2,1)} %movie.1, bf16[64,256,384]{2,1,0:T(8,128)(2,1)} %foot.1, s32[8,384]{1,0:T(8,128)} %support.1, bf16[32,384]{1,0:T(8,128)(2,1)} %bitcast.4, f32[64,256]{1,0:T(8,128)} %weight.1, s32[2,64]{1,0:T(2,128)} %bitcast.5), custom_call_target="tpu_custom_call" | custom-call | tf_op jit(solution)/shard_map/alternation/pallas_call | solution.py:383
  54.3 1.2 %write_out.1 = (f32[32,384]{1,0:T(8,128)}, f32[384,384]{1,0:T(8,128)}, bf16[2048,256]{1,0:T(8,128)(2,1)}) custom-call(f32[32,384]{1,0:T(8,128)S(1)} %get-tuple-element.9.state, f32[384,384]{1,0:T(8,128)S(1)} %get-tuple-element.10.gram, bf16[2048,256]{1,0:T(8,128)(2,1)S(1)} %get-tuple-element.11.rest), custom_call_target="tpu_custom_call" | custom-call | tf_op jit(solution)/shard_map/write_out/pallas_call | solution.py:421
